TPU v7x, 32 devices: a whole 2x2x4 slice. The times are simulated.
32 devices in a mesh: req: 4 (over z), mlp: 8 (over y, x, core).
Axes of the slice: x: 2, y: 2, z: 4, core: 2. Of those that a mesh axis runs over, the one named last changes fastest.
Arguments:
- tokens: bfloat16 [2048, 5120], P(('req', 'mlp')), may hold values from -6 to 6
- norm_scale: float32 [5120], replicated, may hold values from 0.25 to 1.75
- gate_matrix: bfloat16 [5120, 14336], P(None, 'mlp'), may hold values from -0.078125 to 0.078125
- up_matrix: bfloat16 [5120, 14336], P(None, 'mlp'), may hold values from -0.078125 to 0.078125
- down_matrix: bfloat16 [14336, 5120], P('mlp', 'req'), may hold values from -0.046875 to 0.046875
- adapter_down_maps: bfloat16 [8, 32, 5120], P('mlp'), may hold values from -0.078125 to 0.078125
- adapter_gate_up_out: bfloat16 [2, 128, 14336], P(None, None, 'mlp'), may hold values from -1.5 to 1.5
- adapter_down_proj_in: bfloat16 [128, 14336], P(None, 'mlp'), may hold values from -0.046875 to 0.046875
- adapter_down_proj_out: bfloat16 [128, 5120], replicated, may hold values from -1.5 to 1.5
- token_adapters: int32 [2048, 1], P(('req', 'mlp')), may hold values from 0 to 7; in each aligned block of 64 rows (0 to 63, 64 to 127, ...) at most 16 rows name the same one
Outputs:
- mixed: bfloat16 [2048, 5120], P(('req', 'mlp'))
Inputs may be any that keep to these rules, and one draw needn't show every extreme that they name: `token_adapters`: among the 64 rows of one device no adapter is named by more than 16 rows, and in every draw some device has an adapter named by exactly 16 of its rows.
All inputs are finite; a program needn't handle non-finite values.
Results may differ from a plain program's by a relative error of at most 0.013.
Values may be sent and summed in bfloat16 or wider, within the bound.
A program may use at most 192 MiB of HBM per device.

v0:
```python
import jax
import jax.numpy as jnp
from jax import lax
from jax.sharding import PartitionSpec as P

CAP = 16
EPS = 1e-06


def normalize(tokens, norm_scale):
    widened = tokens.astype(jnp.float32)
    mean_square = jnp.mean(widened * widened, axis=-1, keepdims=True)
    return (widened * lax.rsqrt(mean_square + EPS) * norm_scale).astype(jnp.bfloat16)


def rank_routed(normed_input, adapter_lookup, adapter_down_maps, owner_list):
    capacity = CAP
    chosen = (adapter_lookup[:, None] == jnp.arange(owner_list, dtype=jnp.int32)[None, :]).astype(
        jnp.int32
    )
    earlier = jnp.cumsum(chosen, axis=0) - chosen
    slot_of = jnp.sum(earlier * chosen, axis=1)
    target = adapter_lookup * capacity + slot_of
    dispatch = (
        jnp.arange(owner_list * capacity, dtype=jnp.int32)[:, None] == target[None, :]
    ).astype(jnp.bfloat16)
    outgoing = jnp.dot(dispatch, normed_input, preferred_element_type=jnp.float32).astype(
        jnp.bfloat16
    )
    outgoing = outgoing.reshape(owner_list, capacity, normed_input.shape[1])
    owner_table = adapter_down_maps[0]
    produced = jnp.einsum(
        "nkd,rd->nkr",
        lax.all_to_all(outgoing, "mlp", split_axis=0, concat_axis=0, tiled=True),
        owner_table,
        preferred_element_type=jnp.float32,
    ).astype(jnp.bfloat16)
    returned = lax.all_to_all(produced, "mlp", split_axis=0, concat_axis=0, tiled=True)
    returned = returned.reshape(owner_list * capacity, returned.shape[2])
    return lax.dot_general(
        dispatch, returned, (((0,), (0,)), ((), ())), preferred_element_type=jnp.float32
    ).astype(jnp.bfloat16)


def per_device(
    tokens,
    norm_scale,
    gate_matrix,
    up_matrix,
    down_matrix,
    adapter_down_maps,
    adapter_gate_up_out,
    adapter_down_proj_in,
    adapter_down_proj_out,
    token_adapters,
):
    owner_list = lax.axis_size("mlp")
    rank_span = adapter_down_maps.shape[1]
    half_rank = rank_span // 2
    normed_input = normalize(tokens, norm_scale)
    adapter_lookup = token_adapters[:, 0]
    gathered = lax.all_gather(normed_input, "mlp", axis=0, tiled=True)
    group_of = lax.all_gather(adapter_lookup, "mlp", axis=0, tiled=True)
    group_rows = gathered.shape[0]
    selector = group_of[:, None] == jnp.arange(owner_list, dtype=jnp.int32)[None, :]
    zero_half = jnp.zeros((), jnp.bfloat16)
    rank_per_token = rank_routed(normed_input, adapter_lookup, adapter_down_maps, owner_list)
    rank_rows = lax.all_gather(rank_per_token, "mlp", axis=0, tiled=True)
    spread = jnp.where(selector[:, :, None], rank_rows[:, None, :], zero_half)
    gate_rank_values = spread[:, :, :half_rank].reshape(group_rows, owner_list * half_rank)
    up_rank_values = spread[:, :, half_rank:].reshape(group_rows, owner_list * half_rank)
    gate_total = jnp.dot(gathered, gate_matrix, preferred_element_type=jnp.float32) + jnp.dot(
        gate_rank_values, adapter_gate_up_out[0], preferred_element_type=jnp.float32
    )
    up_total = jnp.dot(gathered, up_matrix, preferred_element_type=jnp.float32) + jnp.dot(
        up_rank_values, adapter_gate_up_out[1], preferred_element_type=jnp.float32
    )
    hidden_state = (jax.nn.silu(gate_total) * up_total).astype(jnp.bfloat16)
    rank_term = lax.dot_general(
        hidden_state,
        adapter_down_proj_in,
        (((1,), (1,)), ((), ())),
        preferred_element_type=jnp.float32,
    )
    picker = jnp.repeat(selector, half_rank, axis=1)
    rank_term = jnp.where(picker, rank_term, jnp.float32(0.0))
    down_term = jnp.dot(
        hidden_state,
        lax.all_gather(down_matrix, "req", axis=1, tiled=True),
        preferred_element_type=jnp.float32,
    )
    projected_down = lax.psum_scatter(
        down_term.astype(jnp.bfloat16), "mlp", scatter_dimension=0, tiled=True
    ).astype(jnp.float32)
    total_rank = lax.psum_scatter(
        rank_term.astype(jnp.bfloat16), "mlp", scatter_dimension=0, tiled=True
    )
    adapter_down_term = jnp.dot(
        total_rank, adapter_down_proj_out, preferred_element_type=jnp.float32
    )
    return (tokens.astype(jnp.float32) + projected_down + adapter_down_term).astype(jnp.bfloat16)


def solution(mesh):
    return jax.shard_map(
        per_device,
        mesh=mesh,
        in_specs=(
            P(("req", "mlp"), None),
            P(),
            P(None, "mlp"),
            P(None, "mlp"),
            P("mlp", "req"),
            P("mlp", None, None),
            P(None, None, "mlp"),
            P(None, "mlp"),
            P(),
            P(("req", "mlp"), None),
        ),
        out_specs=P(("req", "mlp"), None),
        check_vma=False,
    )
```

profile of v0, /device:TPU:0, one launch (start us, length us, event | category | flops | bytes accessed | tf_op | source)
XLA Modules:
  0.0 487.8 jit_solution(2720626967359429223)
XLA Ops:
  6.5 1.4 fusion.1
  8.0 2.2 fusion.3
  10.2 0.7 all-gather.7.cloned.1.call-update
  11.1 0.6 dynamic-slice
  12.7 1.5 convolution_convert_fusion.1
  14.2 5.2 %all-to-all-start = ((bf16[8,16,5120]{2,1,0:T(8,128)(2,1)}), bf16[8,16,5120]{2,1,0:T(8,128)(2,1)S(1)}, u32[]{:S(2)}, u32[]{:S(2)}) async-start(bf16[8,16,5120]{2,1,0:T(8,128)(2,1)} %bitcast.2), calls=%async_computation | async-start | bytes 2621440 | tf_op jit(solution)/shard_map/all_to_all | solution.py:34
  19.4 27.4 %all-reduce = s32[512]{0:T(512)S(1)} all-reduce(s32[512]{0:T(512)S(1)} %get-tuple-element.8), channel_id=2, replica_groups=mesh['req'=4,'mlp'=8] {'mlp'}, use_global_device_ids=true, to_apply=%add | all-reduce | flops 512 | bytes 4096
  46.9 2.1 convolution_convert_fusion.2
  48.9 1.5 reshape.71
  50.4 3.3 all-to-all-start.1
  53.9 4.5 all-to-all-done.1
  58.4 0.2 fusion.5
  58.6 8.4 %all-gather.1 = bf16[8,64,32]{1,2,0:T(8,128)(2,1)S(1)} all-gather(bf16[1,64,32]{1,2,0:T(8,128)(2,1)S(1)} %fusion.5), channel_id=1, replica_groups=mesh['req'=4,'mlp'=8] {'mlp'}, dimensions={0}, use_global_device_ids=true | all-gather | bytes 36864 | tf_op jit(solution)/shard_map/all_gather | solution.py:68
  67.3 2.6 fusion.6
  69.8 2.4 fusion.8
  72.3 17.4 %fusion.17 = f32[512,1792]{1,0:T(8,128)} fusion(bf16[512,5120]{1,0:T(8,128)(2,1)} %all-gather.5.cloned.1.call-done, bf16[5120,1792]{1,0:T(8,128)(2,1)} %param.12), kind=kOutput, calls=%fused_computation.35 | convolution fusion | flops 9395240960 | bytes 27262976 | tf_op jit(solution)/shard_map/dot_general | solution.py:72
  89.7 17.4 %multiply_convert_fusion = bf16[512,1792]{1,0:T(8,128)(2,1)S(1)} fusion(f32[512,1792]{1,0:T(8,128)S(1)} %copy-done.3, f32[512,1792]{1,0:T(8,128)} %fusion.17, f32[512,1792]{1,0:T(8,128)S(1)} %copy-done.4, bf16[512,5120]{1,0:T(8,128)(2,1)} %all-gather.5.cloned.1.call-done, bf16[5120,1792]{1,0:T(8,128)(2,1)} %param.13), kind=kOutput, calls=%fused_computation.4 | convolution fusion | flops 9402580992 | bytes 36438016 | tf_op jit(solution)/shard_map/dot_general | solution.py:75
  107.1 1.3 fusion.4
  108.4 0.3 reduce-scatter.5.cloned.1.call-start
  108.7 274.7 %all-gather.7.cloned.1.call-done = bf16[1792,5120]{1,0:T(8,128)(2,1)} async-done(((bf16[1792,1280]{1,0:T(8,128)(2,1)}), bf16[1792,5120]{1,0:T(8,128)(2,1)}) %all-gather.7.cloned.1.call-update) | async-done | bytes 18350096 | tf_op jit(solution)/shard_map/all_gather | solution.py:89
  383.4 15.0 %convolution_convert_fusion = bf16[512,5120]{1,0:T(8,128)(2,1)} fusion(bf16[512,1792]{1,0:T(8,128)(2,1)S(1)} %multiply_convert_fusion, bf16[1792,5120]{1,0:T(8,128)(2,1)} %all-gather.7.cloned.1.call-done), kind=kOutput, calls=%fused_computation | convolution fusion | flops 9397862400 | bytes 25427968 | tf_op jit(solution)/shard_map/dot_general | solution.py:87
  398.4 20.3 %reduce-scatter.7.cloned.1.call-done = bf16[64,128]{1,0:T(8,128)(2,1)} async-done(((bf16[512,128]{1,0:T(8,128)(2,1)}), bf16[64,128]{1,0:T(8,128)(2,1)}) %reduce-scatter.7.cloned.1.call-update) | async-done | bytes 16400
  418.7 60.3 %reduce-scatter.5.cloned.1.call-done = bf16[64,5120]{1,0:T(8,128)(2,1)} async-done(((bf16[512,5120]{1,0:T(8,128)(2,1)}), bf16[64,5120]{1,0:T(8,128)(2,1)}) %reduce-scatter.5.cloned.1.call-update) | async-done | bytes 655376 | tf_op jit(solution)/shard_map/reduce_scatter | solution.py:92
  479.0 2.3 fusion
  (40 shorter events, 1.1 us)
Async XLA Ops:
  6.5 472.4 %copy-start = (bf16[128,5120]{1,0:T(8,128)(2,1)S(1)}, bf16[128,5120]{1,0:T(8,128)(2,1)}, u32[]{:S(2)}) copy-start(bf16[128,5120]{1,0:T(8,128)(2,1)} %param.18) | copy-start | bytes 3932164
  6.5 4.6 copy-start.8
  6.5 4.4 copy-start.7
  6.5 65.7 %all-gather.5.cloned.1.call-start = ((), (), s32[]{:S(2)}) async-start(), calls=%async_computation.4 | async-start | bytes 5898240 | tf_op jit(solution)/shard_map/all_gather | solution.py:62
  10.2 2.5 copy-start.1
  10.2 373.2 %all-gather.7.cloned.1.call-start = ((), (), s32[]{:S(2)}) async-start(), calls=%async_computation.5 | async-start | bytes 22937600 | tf_op jit(solution)/shard_map/all_gather | solution.py:89
  12.7 54.6 %copy-start.5 = (bf16[2,128,1792]{2,1,0:T(8,128)(2,1)S(1)}, bf16[2,128,1792]{2,1,0:T(8,128)(2,1)}, u32[]{:S(2)}) copy-start(bf16[2,128,1792]{2,1,0:T(8,128)(2,1)} %param.16) | copy-start | bytes 2752516
  14.2 32.6 %all-to-all-start = ((bf16[8,16,5120]{2,1,0:T(8,128)(2,1)}), bf16[8,16,5120]{2,1,0:T(8,128)(2,1)S(1)}, u32[]{:S(2)}, u32[]{:S(2)}) async-start(bf16[8,16,5120]{2,1,0:T(8,128)(2,1)} %bitcast.2), calls=%async_computation | async-start | bytes 2621440 | tf_op jit(solution)/shard_map/all_to_all | solution.py:34
  50.4 8.0 %all-to-all-start.1 = ((bf16[8,2,256]{2,1,0:T(2,128)(2,1)}), bf16[8,2,256]{2,1,0:T(2,128)(2,1)S(1)}, u32[]{:S(2)}, u32[]{:S(2)}) async-start(bf16[8,2,256]{2,1,0:T(2,128)(2,1)} %reshape.71), calls=%async_computation.1 | async-start | bytes 16384 | tf_op jit(solution)/shard_map/all_to_all | solution.py:38
  53.6 365.0 %reduce-scatter.7.cloned.1.call-start = ((), (), s32[]{:S(2)}) async-start(), calls=%async_computation.7 | async-start | bytes 147456
  72.3 17.4 %copy-start.3 = (f32[512,1792]{1,0:T(8,128)S(1)}, f32[512,1792]{1,0:T(8,128)}, u32[]{:S(2)}) copy-start(f32[512,1792]{1,0:T(8,128)} %fusion.6) | copy-start | bytes 11010052
  72.3 17.4 %copy-start.4 = (f32[512,1792]{1,0:T(8,128)S(1)}, f32[512,1792]{1,0:T(8,128)}, u32[]{:S(2)}) copy-start(f32[512,1792]{1,0:T(8,128)} %fusion.8) | copy-start | bytes 11010052
  89.7 17.4 %copy-start.6 = (bf16[128,1792]{1,0:T(8,128)(2,1)S(1)}, bf16[128,1792]{1,0:T(8,128)(2,1)}, u32[]{:S(2)}) copy-start(bf16[128,1792]{1,0:T(8,128)(2,1)} %param.17) | copy-start | bytes 1376260
  108.4 370.5 %reduce-scatter.5.cloned.1.call-start = ((), (), s32[]{:S(2)}) async-start(), calls=%async_computation.6 | async-start | bytes 5898240 | tf_op jit(solution)/shard_map/reduce_scatter | solution.py:92
  398.4 80.6 %copy-start.2 = (bf16[64,5120]{1,0:T(8,128)(2,1)S(1)}, bf16[64,5120]{1,0:T(8,128)(2,1)}, u32[]{:S(2)}) copy-start(bf16[64,5120]{1,0:T(8,128)(2,1)} %param.10) | copy-start | bytes 1966084
Sparse Core Ops, SparseCore 0:
  10.3 57.3 all-gather.4
  69.3 314.0 all-gather.6
  386.4 32.2 reduce-scatter.6
  422.3 56.6 reduce-scatter.4
where the time goes:
time: 488 us
  waiting for transfers between devices  360 us (74%)
  matrix products  62.2 us (13%)
  blocking collectives  35.9 us (7%)
  between operations  13.9 us (3%)
  starting transfers between devices  8.78 us (2%)
    all_gather x1, waiting for transfers between devices, per_device(): lax.all_gather(down_matrix, 'req', axis=1, tiled=True)  275 us
    reduce_scatter x1, waiting for transfers between devices, per_device(): lax.psum_scatter(down_term.astype(jnp.bfloat16), 'mlp', scatter_dimension...  60.3 us
    unnamed x1, blocking collectives  27.4 us
    unnamed x5, waiting for transfers between devices  21 us
    dot_general x1, matrix products, per_device(): jnp.dot(gathered, gate_matrix, preferred_element_type=jnp.float32)  17.4 us
    dot_general x1, matrix products, per_device(): jnp.dot(gathered, up_matrix, preferred_element_type=jnp.float32)  17.4 us
    dot_general x1, matrix products, per_device(): jnp.dot(hidden_state, lax.all_gather(down_matrix, 'req', axis=1, tiled=Tr...  15 us
  transfers between devices with their start and end apart: 6, of which 4 were waited for; matrix products, arithmetic and copies ran while one was open for 13% of the time, Pallas kernels for 0%

commit v1 on v0

--- a/solution.py
+++ b/solution.py
@@ -1,10 +1,42 @@
+import functools
 import jax
 import jax.numpy as jnp
 from jax import lax
 from jax.sharding import PartitionSpec as P
+from jax.lax import axis_index, ppermute, psum
 
 CAP = 16
 EPS = 1e-06
+
+
+def lift_sheets_on(a0, dim_i, across):
+    ready = psum(1, across)
+    raw_out = axis_index(across)
+    latest, a_next, block_last = (ready, raw_out, a0.shape[dim_i])
+    tray = [p * latest if i == dim_i else p for i, p in enumerate(a0.shape)]
+    carry_out = jnp.zeros(tray, a0.dtype)
+    next_value = lax.dynamic_update_slice_in_dim(carry_out, a0, a_next * block_last, axis=dim_i)
+    last = x_new = a0
+    for i0 in range(1, latest // 2 + 1):
+        mat_out = range(latest)
+        odd = map(lambda i: (i, (i + 1) % latest), mat_out)
+        heard = list(odd)
+        last = ppermute(last, across, perm=heard)
+        next_value = lax.dynamic_update_slice_in_dim(
+            next_value, last, (a_next - i0) % latest * block_last, axis=dim_i
+        )
+        if 2 * i0 < latest:
+            w2 = range(latest)
+            found_now = map(lambda i: (i, (i - 1) % latest), w2)
+            u_next = list(found_now)
+            x_new = ppermute(x_new, across, u_next)
+            next_value = lax.dynamic_update_slice_in_dim(
+                next_value, x_new, (a_next + i0) % latest * block_last, axis=dim_i
+            )
+    return next_value
+
+
+register_the_cycles = functools.partial(lift_sheets_on, dim_i=1, across="req")
 
 
 def normalize(tokens, norm_scale):
@@ -85,9 +117,7 @@
     picker = jnp.repeat(selector, half_rank, axis=1)
     rank_term = jnp.where(picker, rank_term, jnp.float32(0.0))
     down_term = jnp.dot(
-        hidden_state,
-        lax.all_gather(down_matrix, "req", axis=1, tiled=True),
-        preferred_element_type=jnp.float32,
+        hidden_state, register_the_cycles(down_matrix), preferred_element_type=jnp.float32
     )
     projected_down = lax.psum_scatter(
         down_term.astype(jnp.bfloat16), "mlp", scatter_dimension=0, tiled=True

time: 488 us -> 396 us (0.81)
  waiting for transfers between devices: 360 us -> 243 us
  local copies, waits for them, and re-layouts: 2.53 us -> 26.8 us
  blocking collectives: 35.9 us -> 29.5 us
    all_gather x1 -> x0, waiting for transfers between devices: 275 us -> none  [per_device(): lax.all_gather(down_matrix, 'req', axis=1, tiled=True)]
    ppermute x0 -> x3, waiting for transfers between devices: none -> 184 us  [the longest x1 92.3 us: lift_sheets_on(): x_new = ppermute(x_new, across, u_next)]
    unnamed x5 -> x4, waiting for transfers between devices: 21 us -> 0.07 us
    dynamic_update_slice x0 -> x4, local copies, waits for them, and re-layouts: none -> 17.1 us  [the longest x2 9.64 us: lift_sheets_on(): lax.dynamic_update_slice_in_dim(next_value, last, (a_next - i0) % latest...]
    broadcast_in_dim x0 -> x1, local copies, waits for them, and re-layouts: none -> 7.3 us  [lift_sheets_on(): carry_out = jnp.zeros(tray, a0.dtype)]
    unnamed x1, blocking collectives: 27.4 us -> 21.2 us
    reduce_scatter x1, waiting for transfers between devices: 60.3 us -> 55 us  [per_device(): lax.psum_scatter(down_term.astype(jnp.bfloat16), 'mlp', scatter_dimension...]
    ppermute x0 -> x3, starting transfers between devices: none -> 5.17 us  [the longest x2 3.08 us: lift_sheets_on(): last = ppermute(last, across, perm=heard)]
  transfers between devices with their start and end apart: 6 -> 8, of which waited for: 4 -> 5; matrix products, arithmetic and copies ran while one was open for 13% -> 23% of each run, Pallas kernels for 0% -> 0%
where the time goes in v1:
time: 396 us
  waiting for transfers between devices  243 us (61%)
  matrix products  61.3 us (15%)
  blocking collectives  29.5 us (7%)
  local copies, waits for them, and re-layouts  26.8 us (7%)
  between operations  14 us (4%)
  starting transfers between devices  12.8 us (3%)
  other arithmetic  8.13 us (2%)
    ppermute x1, waiting for transfers between devices, lift_sheets_on(): x_new = ppermute(x_new, across, u_next)  92.3 us
    ppermute x2, waiting for transfers between devices, lift_sheets_on(): last = ppermute(last, across, perm=heard)  91.7 us
    reduce_scatter x1, waiting for transfers between devices, per_device(): lax.psum_scatter(down_term.astype(jnp.bfloat16), 'mlp', scatter_dimension...  55 us
    unnamed x1, blocking collectives  21.2 us
    dot_general x1, matrix products, per_device(): jnp.dot(gathered, up_matrix, preferred_element_type=jnp.float32)  17.3 us
    dot_general x1, matrix products, per_device(): jnp.dot(gathered, gate_matrix, preferred_element_type=jnp.float32)  16.2 us
    dot_general x1, matrix products, per_device(): jnp.dot(hidden_state, register_the_cycles(down_matrix), preferred_element...  14.9 us
    dynamic_update_slice x2, local copies, waits for them, and re-layouts, lift_sheets_on(): lax.dynamic_update_slice_in_dim(next_value, last, (a_next - i0) % latest...  9.64 us
  transfers between devices with their start and end apart: 8, of which 5 were waited for; matrix products, arithmetic and copies ran while one was open for 23% of the time, Pallas kernels for 0%

profile of v1, /device:TPU:0, one launch (start us, length us, event | category | flops | bytes accessed | tf_op | source)
XLA Modules:
  0.0 395.8 jit_solution(16940935980259489717)
XLA Ops:
  8.0 2.2 fusion.2
  10.2 3.1 collective-permute-start
  13.2 2.1 collective-permute-start.1
  19.6 2.7 convolution_convert_fusion.1
  22.4 4.0 %all-to-all-start = ((bf16[8,16,5120]{2,1,0:T(8,128)(2,1)}), bf16[8,16,5120]{2,1,0:T(8,128)(2,1)S(1)}, u32[]{:S(2)}, u32[]{:S(2)}) async-start(bf16[8,16,5120]{2,1,0:T(8,128)(2,1)} %bitcast.2), calls=%async_computation | async-start | bytes 2621440 | tf_op jit(solution)/shard_map/all_to_all | solution.py:66
  26.4 21.2 %all-reduce = s32[512]{0:T(512)S(1)} all-reduce(s32[512]{0:T(512)S(1)} %get-tuple-element.8), channel_id=2, replica_groups=mesh['req'=4,'mlp'=8] {'mlp'}, use_global_device_ids=true, to_apply=%add | all-reduce | flops 512 | bytes 4096
  47.6 7.3 %broadcast_in_dim.42 = bf16[1792,5120]{1,0:T(8,128)(2,1)} broadcast(bf16[]{:T(256)} %constant.47.clone.1), dimensions={} | broadcast | bytes 18350082 | tf_op jit(solution)/shard_map/broadcast_in_dim | solution.py:17
  54.9 2.6 constant_dynamic-update-slice_fusion.3
  58.7 3.3 all-to-all-start.1
  62.3 4.3 %all-to-all-done.1 = bf16[8,2,256]{2,1,0:T(2,128)(2,1)S(1)} async-done(((bf16[8,2,256]{2,1,0:T(2,128)(2,1)}), bf16[8,2,256]{2,1,0:T(2,128)(2,1)S(1)}, u32[]{:S(2)}, u32[]{:S(2)}) %all-to-all-start.1) | async-done | bytes 8224 | tf_op jit(solution)/shard_map/all_to_all | solution.py:70
  66.9 8.3 %all-gather.1 = bf16[8,64,32]{1,2,0:T(8,128)(2,1)S(1)} all-gather(bf16[1,64,32]{1,2,0:T(8,128)(2,1)S(1)} %fusion.6), channel_id=1, replica_groups=mesh['req'=4,'mlp'=8] {'mlp'}, dimensions={0}, use_global_device_ids=true | all-gather | bytes 36864 | tf_op jit(solution)/shard_map/all_gather | solution.py:100
  75.4 3.5 fusion.7
  78.9 3.5 fusion.9
  82.4 33.0 %collective-permute-done = bf16[1792,1280]{1,0:T(8,128)(2,1)} collective-permute-done((bf16[1792,1280]{1,0:T(8,128)(2,1)}, bf16[1792,1280]{1,0:T(8,128)(2,1)}, u32[]{:S(2)}, u32[]{:S(2)}) %collective-permute-start) | collective-permute-done | bytes 4587552 | tf_op jit(solution)/shard_map/ppermute | solution.py:24
  115.4 4.8 %constant_dynamic-update-slice_fusion.2 = bf16[1792,5120]{1,0:T(8,128)(2,1)} fusion(bf16[1792,5120]{1,0:T(8,128)(2,1)} %constant_dynamic-update-slice_fusion.3, bf16[1792,1280]{1,0:T(8,128)(2,1)} %collective-permute-done, s32[]{:T(128)S(6)} %select_n.38), kind=kLoop, calls=%fused_computation.33 | loop fusion | bytes 9175044 | tf_op jit(solution)/shard_map/dynamic_update_slice | solution.py:25
  120.3 92.3 %collective-permute-done.1 = bf16[1792,1280]{1,0:T(8,128)(2,1)} collective-permute-done((bf16[1792,1280]{1,0:T(8,128)(2,1)}, bf16[1792,1280]{1,0:T(8,128)(2,1)}, u32[]{:S(2)}, u32[]{:S(2)}) %collective-permute-start.1) | collective-permute-done | bytes 4587552 | tf_op jit(solution)/shard_map/ppermute | solution.py:32
  212.5 4.9 %constant_dynamic-update-slice_fusion.1 = bf16[1792,5120]{1,0:T(8,128)(2,1)} fusion(bf16[1792,5120]{1,0:T(8,128)(2,1)} %constant_dynamic-update-slice_fusion.2, bf16[1792,1280]{1,0:T(8,128)(2,1)} %collective-permute-done.1, s32[]{:T(128)S(6)} %select_n.40), kind=kLoop, calls=%fused_computation.32 | loop fusion | bytes 9175044 | tf_op jit(solution)/shard_map/dynamic_update_slice | solution.py:33
  217.4 16.2 %fusion.18 = f32[512,1792]{1,0:T(8,128)} fusion(bf16[512,5120]{1,0:T(8,128)(2,1)} %all-gather.4.cloned.1.call-done, bf16[5120,1792]{1,0:T(8,128)(2,1)} %param.12), kind=kOutput, calls=%fused_computation.39 | convolution fusion | flops 9395240960 | bytes 27262976 | tf_op jit(solution)/shard_map/dot_general | solution.py:104
  233.7 17.3 %multiply_convert_fusion = bf16[512,1792]{1,0:T(8,128)(2,1)S(1)} fusion(f32[512,1792]{1,0:T(8,128)S(1)} %copy-done.2, f32[512,1792]{1,0:T(8,128)} %fusion.18, f32[512,1792]{1,0:T(8,128)S(1)} %copy-done.3, bf16[512,5120]{1,0:T(8,128)(2,1)} %all-gather.4.cloned.1.call-done, bf16[5120,1792]{1,0:T(8,128)(2,1)} %param.13), kind=kOutput, calls=%fused_computation.2 | convolution fusion | flops 9402580992 | bytes 36438016 | tf_op jit(solution)/shard_map/dot_general | solution.py:107
  252.6 58.7 %collective-permute-done.2 = bf16[1792,1280]{1,0:T(8,128)(2,1)} collective-permute-done((bf16[1792,1280]{1,0:T(8,128)(2,1)}, bf16[1792,1280]{1,0:T(8,128)(2,1)}, u32[]{:S(2)}, u32[]{:S(2)}) %collective-permute-start.2) | collective-permute-done | bytes 4587552 | tf_op jit(solution)/shard_map/ppermute | solution.py:24
  311.2 4.8 %constant_dynamic-update-slice_fusion = bf16[1792,5120]{1,0:T(8,128)(2,1)} fusion(bf16[1792,5120]{1,0:T(8,128)(2,1)} %constant_dynamic-update-slice_fusion.1, bf16[1792,1280]{1,0:T(8,128)(2,1)} %collective-permute-done.2, s32[]{:T(128)S(6)} %select_n.42), kind=kLoop, calls=%fused_computation.31 | loop fusion | bytes 9175044 | tf_op jit(solution)/shard_map/dynamic_update_slice | solution.py:25
  316.1 14.9 %convolution_convert_fusion = bf16[512,5120]{1,0:T(8,128)(2,1)} fusion(bf16[512,1792]{1,0:T(8,128)(2,1)S(1)} %multiply_convert_fusion, bf16[1792,5120]{1,0:T(8,128)(2,1)} %constant_dynamic-update-slice_fusion), kind=kOutput, calls=%fused_computation | convolution fusion | flops 9397862400 | bytes 25427968 | tf_op jit(solution)/shard_map/dot_general | solution.py:119
  332.1 55.0 %reduce-scatter.5.cloned.1.call-done = bf16[64,5120]{1,0:T(8,128)(2,1)} async-done(((bf16[512,5120]{1,0:T(8,128)(2,1)}), bf16[64,5120]{1,0:T(8,128)(2,1)}) %reduce-scatter.5.cloned.1.call-update) | async-done | bytes 655376 | tf_op jit(solution)/shard_map/reduce_scatter | solution.py:122
  387.1 2.1 fusion.4
  (48 shorter events, 9.7 us)
Async XLA Ops:
  6.5 324.5 %copy-start = (bf16[128,5120]{1,0:T(8,128)(2,1)S(1)}, bf16[128,5120]{1,0:T(8,128)(2,1)}, u32[]{:S(2)}) copy-start(bf16[128,5120]{1,0:T(8,128)(2,1)} %param.18) | copy-start | bytes 3932164
  6.5 210.9 %all-gather.4.cloned.1.call-start = ((), (), s32[]{:S(2)}) async-start(), calls=%async_computation.4 | async-start | bytes 5898240 | tf_op jit(solution)/shard_map/all_gather | solution.py:94
  10.2 105.3 %collective-permute-start = (bf16[1792,1280]{1,0:T(8,128)(2,1)}, bf16[1792,1280]{1,0:T(8,128)(2,1)}, u32[]{:S(2)}, u32[]{:S(2)}) collective-permute-start(bf16[1792,1280]{1,0:T(8,128)(2,1)} %param.14), channel_id=1, source_target_pairs={{0,8},{8,16},{16,24},{24,0},{1,9},{9,17},{17,25},{25,1},{2,10},{10... | collective-permute-start | bytes 13762568 | tf_op jit(solution)/shard_map/ppermute | solution.py:24
  13.2 199.3 %collective-permute-start.1 = (bf16[1792,1280]{1,0:T(8,128)(2,1)}, bf16[1792,1280]{1,0:T(8,128)(2,1)}, u32[]{:S(2)}, u32[]{:S(2)}) collective-permute-start(bf16[1792,1280]{1,0:T(8,128)(2,1)} %param.14), channel_id=1, source_target_pairs={{0,24},{8,0},{16,8},{24,16},{1,25},{9,1},{17,9},{25,17},{2,26},{10... | collective-permute-start | bytes 13762568 | tf_op jit(solution)/shard_map/ppermute | solution.py:32
  22.4 32.5 %slice-start = ((s8[4587520]{0:T(1024)(128)(4,1)}), s8[393216]{0:T(1024)(128)(4,1)S(1)}, s32[]{:S(2)}) async-start(s8[4587520]{0:T(1024)(128)(4,1)} %bitcast.39), calls=%async_computation.7 | async-start | bytes 786432
  22.4 35.1 %all-to-all-start = ((bf16[8,16,5120]{2,1,0:T(8,128)(2,1)}), bf16[8,16,5120]{2,1,0:T(8,128)(2,1)S(1)}, u32[]{:S(2)}, u32[]{:S(2)}) async-start(bf16[8,16,5120]{2,1,0:T(8,128)(2,1)} %bitcast.2), calls=%async_computation | async-start | bytes 2621440 | tf_op jit(solution)/shard_map/all_to_all | solution.py:66
  47.6 7.3 %slice-start.1 = ((s8[4587520]{0:T(1024)(128)(4,1)}), s8[4194304]{0:T(1024)(128)(4,1)S(1)}, s32[]{:S(2)}) async-start(s8[4587520]{0:T(1024)(128)(4,1)} %bitcast.39), calls=%async_computation.8 | async-start | bytes 8388608
  54.9 2.6 copy-start.5
  58.7 8.0 %all-to-all-start.1 = ((bf16[8,2,256]{2,1,0:T(2,128)(2,1)}), bf16[8,2,256]{2,1,0:T(2,128)(2,1)S(1)}, u32[]{:S(2)}, u32[]{:S(2)}) async-start(bf16[8,2,256]{2,1,0:T(2,128)(2,1)} %reshape.71), calls=%async_computation.1 | async-start | bytes 16384 | tf_op jit(solution)/shard_map/all_to_all | solution.py:70
  62.0 269.0 %reduce-scatter.7.cloned.1.call-start = ((), (), s32[]{:S(2)}) async-start(), calls=%async_computation.6 | async-start | bytes 147456
  115.4 195.8 %collective-permute-start.2 = (bf16[1792,1280]{1,0:T(8,128)(2,1)}, bf16[1792,1280]{1,0:T(8,128)(2,1)}, u32[]{:S(2)}, u32[]{:S(2)}) collective-permute-start(bf16[1792,1280]{1,0:T(8,128)(2,1)} %collective-permute-done), channel_id=1, source_target_pairs={{0,8},{8,16},{16,24},{24,0},{1,9},{9,17},{17,25},{25,1},{2,10},{10... | collective-permute-start | bytes 13762568 | tf_op jit(solution)/shard_map/ppermute | solution.py:24
  217.4 16.2 %copy-start.2 = (f32[512,1792]{1,0:T(8,128)S(1)}, f32[512,1792]{1,0:T(8,128)}, u32[]{:S(2)}) copy-start(f32[512,1792]{1,0:T(8,128)} %fusion.7) | copy-start | bytes 11010052
  217.4 16.2 %copy-start.3 = (f32[512,1792]{1,0:T(8,128)S(1)}, f32[512,1792]{1,0:T(8,128)}, u32[]{:S(2)}) copy-start(f32[512,1792]{1,0:T(8,128)} %fusion.9) | copy-start | bytes 11010052
  233.6 17.3 %copy-start.4 = (bf16[128,1792]{1,0:T(8,128)(2,1)S(1)}, bf16[128,1792]{1,0:T(8,128)(2,1)}, u32[]{:S(2)}) copy-start(bf16[128,1792]{1,0:T(8,128)(2,1)} %param.17) | copy-start | bytes 1376260
  252.3 134.8 %reduce-scatter.5.cloned.1.call-start = ((), (), s32[]{:S(2)}) async-start(), calls=%async_computation.5 | async-start | bytes 5898240 | tf_op jit(solution)/shard_map/reduce_scatter | solution.py:122
  331.0 56.2 %copy-start.1 = (bf16[64,5120]{1,0:T(8,128)(2,1)S(1)}, bf16[64,5120]{1,0:T(8,128)(2,1)}, u32[]{:S(2)}) copy-start(bf16[64,5120]{1,0:T(8,128)(2,1)} %param.10) | copy-start | bytes 1966084
Sparse Core Ops, SparseCore 0:
  10.3 50.9 all-gather.3
  252.4 37.4 reduce-scatter.6
  331.1 55.9 reduce-scatter.4
